TPU v7x, 128 devices: a whole 4x4x4 slice. The times are simulated.
128 devices in a mesh: blk: 16 (over x_hi, z, core), tile: 8 (over x_lo, y).
Axes of the slice: x: 4 (x_hi: 2, x_lo: 2; x = x_hi * 2 + x_lo), y: 4, z: 4, core: 2. Of those that a mesh axis runs over, the one named last changes fastest.
Arguments:
- features: bfloat16 [8192, 8192], P('tile', 'blk'), may hold values from -6 to 6
- weight_kv: bfloat16 [8192, 12288], P(None, 'blk'), may hold values from -0.0625 to 0.0625
- key_gain: float32 [6, 128], replicated, may hold values from 0.1 to 1.9
- block_reader: int32 [64], P('tile'), may hold values from 0 to 7, as said below
Outputs:
- routed_kv: bfloat16 [32768, 12288], P('tile', 'blk')
Inputs may be any that keep to these rules, and one draw needn't show every extreme that they name: `block_reader`: at most 4 of the 8 blocks of one index of tile name the same reader, and one reader is named by exactly 4 blocks of every index of tile.
All inputs are finite; a program needn't handle non-finite values.
Results may differ from a plain program's by a relative error of at most 0.001.
Values may be sent and summed in bfloat16 or wider, within the bound.
A program may use at most 192 MiB of HBM per device.

v0:
```python
import jax
import jax.numpy as jnp
from jax import lax
from jax.sharding import PartitionSpec as P

KVH = 8
HD = 128
L = 6
BT = 128
CAP = 4
norm_eps = 1e-05


def local_slots(readers, tile_count):
    onehot = (readers[:, None] == jnp.arange(tile_count, dtype=jnp.int32)[None, :]).astype(
        jnp.int32
    )
    earlier = jnp.cumsum(onehot, axis=0) - onehot
    slot_rank = jnp.sum(earlier * onehot, axis=1)
    return readers * CAP + slot_rank


def shards(features, weight_kv, key_gain, block_reader):
    row_count, feat_local = features.shape
    col_count = weight_kv.shape[1]
    pair_count = col_count // (2 * HD)
    tile_count = lax.axis_size("tile")
    block_count = row_count // BT
    layer_ids = (
        lax.axis_index("blk") * pair_count + jnp.arange(pair_count, dtype=jnp.int32)
    ) // KVH
    layer_pick = (layer_ids[:, None] == jnp.arange(L, dtype=jnp.int32)[None, :]).astype(jnp.float32)
    key_gains = jnp.dot(layer_pick, key_gain, precision=lax.Precision.HIGHEST)
    slot_index = local_slots(block_reader, tile_count)
    selector = (
        slot_index[None, :] == jnp.arange(tile_count * CAP, dtype=jnp.int32)[:, None]
    ).astype(jnp.bfloat16)
    slot_rows = tile_count * CAP * BT
    running = jnp.dot(
        lax.all_gather(features, "blk", axis=1, tiled=True),
        weight_kv,
        preferred_element_type=jnp.float32,
    )
    count = running.shape[0]
    halves = running.reshape(count, pair_count, 2, HD)
    key_part = halves[:, :, 0]
    mean_square = jnp.mean(key_part * key_part, axis=-1, keepdims=True)
    key_part = key_part * lax.rsqrt(mean_square + norm_eps) * key_gains[None]
    joined = jnp.stack([key_part, halves[:, :, 1]], axis=2)
    key_value = joined.reshape(count, col_count).astype(jnp.bfloat16)
    outgoing = jnp.dot(
        selector, key_value.reshape(block_count, BT * col_count), preferred_element_type=jnp.float32
    )
    outgoing = outgoing.astype(jnp.bfloat16).reshape(slot_rows, col_count)
    routed = lax.all_to_all(outgoing, "tile", split_axis=0, concat_axis=0, tiled=True)
    return routed


def solution(mesh):
    return jax.shard_map(
        shards,
        mesh=mesh,
        in_specs=(P("tile", "blk"), P(None, "blk"), P(), P("tile")),
        out_specs=P("tile", "blk"),
        check_vma=False,
    )
```

profile of v0, /device:TPU:0, one launch (start us, length us, event | category | flops | bytes accessed | tf_op | source)
XLA Modules:
  0.0 278.6 jit_solution(7639619202823156865)
XLA Ops:
  6.5 0.0 copy-start
  6.5 0.0 all-gather.2.cloned.1.call-start
  6.5 0.7 all-gather.2.cloned.1.call-update
  7.3 0.7 fusion.1
  8.0 0.8 select_reduce_fusion
  8.9 0.7 multiply_add_fusion
  9.5 0.0 copy-done
  9.5 0.2 fusion.2
  9.7 121.5 %all-gather.2.cloned.1.call-done = bf16[1024,8192]{1,0:T(8,128)(2,1)} async-done(((bf16[1024,512]{1,0:T(8,128)(2,1)}), bf16[1024,8192]{1,0:T(8,128)(2,1)}) %all-gather.2.cloned.1.call-update) | async-done | bytes 16777232 | tf_op jit(solution)/shard_map/all_gather | solution.py:40
  131.2 20.3 %fusion.4 = f32[1024,768]{0,1:T(8,128)} fusion(bf16[1024,8192]{1,0:T(8,128)(2,1)} %all-gather.2.cloned.1.call-done, bf16[8192,768]{1,0:T(8,128)(2,1)} %param.5), kind=kOutput, calls=%fused_computation.18 | convolution fusion | flops 12884901888 | bytes 32505856 | tf_op jit(solution)/shard_map/dot_general | solution.py:39
  151.5 1.5 slice.9
  153.0 2.4 slice.10
  155.4 1.7 copy.16
  157.2 5.7 %multiply_reduce_fusion = f32[1024,3]{1,0:T(8,128)S(1)} fusion(f32[1024,3,1,128]{3,2,1,0:T(1,128)S(1)} %copy.16), kind=kLoop, calls=%fused_computation.3 | loop fusion | flops 783360 | bytes 1585152 | tf_op jit(solution)/shard_map/reduce_sum | solution.py:47
  162.9 0.9 add_rsqrt_fusion
  163.8 4.1 %copy.17 = bf16[1024,3,1,128]{3,2,1,0:T(2,128)(2,1)S(1)} copy(bf16[1024,3,1,128]{0,3,2,1:T(8,128)(2,1)} %slice.10) | data formatting | bytes 1572864
  167.9 8.0 %multiply_convert_fusion = bf16[1024,3,1,128]{3,2,1,0:T(2,128)(2,1)S(1)} fusion(f32[1024,3,1,128]{3,2,1,0:T(1,128)S(1)} %copy.16, f32[3,128]{1,0:T(4,128)S(1)} %fusion.2, f32[1024,3]{1,0:T(8,128)} %add_rsqrt_fusion), kind=kLoop, calls=%fused_computation.2 | loop fusion | flops 1179648 | bytes 2373120 | tf_op jit(solution)/shard_map/convert
  176.0 3.6 %pad_maximum_fusion = bf16[1024,3,2,128]{3,2,1,0:T(2,128)(2,1)S(1)} fusion(bf16[1024,3,1,128]{3,2,1,0:T(2,128)(2,1)S(1)} %copy.17, bf16[1024,3,1,128]{3,2,1,0:T(2,128)(2,1)S(1)} %multiply_convert_fusion), kind=kLoop, calls=%fused_computation.1 | loop fusion | flops 3145728 | bytes 3145728 | tf_op jit(solution)/shard_map/stack | solution.py:49
  179.6 1.2 convert_element_type.14
  180.8 4.5 %convolution_convert_fusion = bf16[32,98304]{1,0:T(8,128)(2,1)} fusion(bf16[8,98304]{1,0:T(8,128)(2,1)S(1)} %convert_element_type.14, s32[8]{0:T(128)S(1)} %multiply_add_fusion), kind=kOutput, calls=%fused_computation | convolution fusion | flops 53477632 | bytes 7864352 | tf_op jit(solution)/shard_map/dot_general | solution.py:51
  185.3 7.3 %all_to_all.8 = bf16[8,512,768]{2,1,0:T(8,128)(2,1)} reshape(bf16[32,98304]{1,0:T(8,128)(2,1)} %convolution_convert_fusion) | data formatting | bytes 12582912 | tf_op jit(solution)/shard_map/all_to_all | solution.py:55
  192.5 76.5 %all_to_all.12 = bf16[8,512,768]{2,1,0:T(8,128)(2,1)S(1)} all-to-all(bf16[8,512,768]{2,1,0:T(8,128)(2,1)} %all_to_all.8), channel_id=1, replica_groups=mesh['blk'=16,'tile'=8] {'tile'}, dimensions={0} | all-to-all | bytes 12582912 | tf_op jit(solution)/shard_map/all_to_all | solution.py:55
  269.1 0.0 copy-start.1
  269.1 2.7 copy.20
  271.8 0.0 copy-done.1
  (2 shorter events, 0.0 us)
Async XLA Ops:
  6.5 3.0 %copy-start = (f32[6,128]{1,0:T(8,128)S(1)}, f32[6,128]{1,0:T(8,128)}, u32[]{:S(2)}) copy-start(f32[6,128]{1,0:T(8,128)} %param.6) | copy-start | bytes 9220
  6.5 124.7 %all-gather.2.cloned.1.call-start = ((), (), s32[]{:S(2)}) async-start(), calls=%async_computation.1 | async-start | bytes 17825792 | tf_op jit(solution)/shard_map/all_gather | solution.py:40
  269.1 2.7 copy-start.1
Sparse Core Ops, SparseCore 0:
  9.6 121.5 all-gather.1
where the time goes:
time: 279 us
  waiting for transfers between devices  122 us (44%)
  blocking collectives  76.5 us (27%)
  matrix products  24.9 us (9%)
  local copies, waits for them, and re-layouts  21 us (8%)
  other arithmetic  20.5 us (7%)
  between operations  13.4 us (5%)
    all_gather x1, waiting for transfers between devices, shards(): lax.all_gather(features, 'blk', axis=1, tiled=True)  122 us
    all_to_all x1, blocking collectives, shards(): lax.all_to_all(outgoing, 'tile', split_axis=0, concat_axis=0, tiled=True)  76.5 us
    dot_general x1, matrix products, shards(): jnp.dot(lax.all_gather(features, 'blk', axis=1, tiled=True), weight_kv, p...  20.3 us
    unnamed x7, local copies, waits for them, and re-layouts  8.58 us
    another operation x1, other arithmetic  8.05 us
    all_to_all x1, local copies, waits for them, and re-layouts, shards(): lax.all_to_all(outgoing, 'tile', split_axis=0, concat_axis=0, tiled=True)  7.28 us
    reduce_sum x1, other arithmetic, shards(): mean_square = jnp.mean(key_part * key_part, axis=-1, keepdims=True)  5.71 us
  transfers between devices with their start and end apart: 1, of which 1 were waited for; matrix products, arithmetic and copies ran while one was open for 1% of the time, Pallas kernels for 0%

commit v1 on v0

--- a/solution.py
+++ b/solution.py
@@ -37,7 +37,9 @@
     ).astype(jnp.bfloat16)
     slot_rows = tile_count * CAP * BT
     running = jnp.dot(
-        lax.all_gather(features, "blk", axis=1, tiled=True),
+        jnp.concatenate(
+            lax.all_to_all(jnp.stack([features] * lax.axis_size("blk")), "blk", 0, 0), axis=1
+        ),
         weight_kv,
         preferred_element_type=jnp.float32,
     )

time: 279 us -> 436 us (1.56); the launches traced: 279 us -> 428 us
  waiting for transfers between devices: 122 us -> 239 us
  local copies, waits for them, and re-layouts: 21 us -> 80.1 us
  other arithmetic: 20.5 us -> 0.82 us
  between operations: 13.4 us -> 0.08 us
  starting transfers between devices: 0.01 us -> 8.01 us
    all_to_all x0 -> x1, waiting for transfers between devices: none -> 239 us  [shards(): lax.all_to_all(jnp.stack([features] * lax.axis_size('blk')), 'blk', 0, 0)]
    all_gather x1 -> x0, waiting for transfers between devices: 122 us -> none  [shards(): lax.all_gather(features, 'blk', axis=1, tiled=True)]
    reshape x0 -> x2, local copies, waits for them, and re-layouts: none -> 44.1 us  [shards(): jnp.concatenate(lax.all_to_all(jnp.stack([features] * lax.axis_size('blk'...]
    dot_general x0 -> x1, local copies, waits for them, and re-layouts: none -> 15.7 us  [shards(): jnp.dot(jnp.concatenate(lax.all_to_all(jnp.stack([features] * lax.axis_si...]
    another operation x0 -> x2, local copies, waits for them, and re-layouts: none -> 9.04 us  [the longest x1 6.81 us: shards(): jnp.stack([features] * lax.axis_size('blk'))]
    all_to_all x0 -> x1, starting transfers between devices: none -> 8.01 us  [shards(): lax.all_to_all(jnp.stack([features] * lax.axis_size('blk')), 'blk', 0, 0)]
    another operation x1, other arithmetic: 8.05 us -> 0.2 us
    unnamed x7, local copies, waits for them, and re-layouts: 8.58 us -> 2.72 us
  transfers between devices with their start and end apart: 1 -> 1, of which waited for: 1 -> 1; matrix products, arithmetic and copies ran while one was open for 1% -> 4% of each run, Pallas kernels for 0% -> 0%
where the time goes in v1:
time: 436 us; the launch traced here: 428 us
  waiting for transfers between devices  239 us (55%)
  local copies, waits for them, and re-layouts  80.1 us (18%)
  blocking collectives  77.1 us (18%)
  matrix products  23.2 us (5%)
  starting transfers between devices  8.01 us (2%)
    all_to_all x1, waiting for transfers between devices, shards(): lax.all_to_all(jnp.stack([features] * lax.axis_size('blk')), 'blk', 0, 0)  239 us
    all_to_all x1, blocking collectives, shards(): lax.all_to_all(outgoing, 'tile', split_axis=0, concat_axis=0, tiled=True)  77.1 us
    reshape x2, local copies, waits for them, and re-layouts, shards(): jnp.concatenate(lax.all_to_all(jnp.stack([features] * lax.axis_size('blk'...  44.1 us
    dot_general x1, matrix products, shards(): jnp.dot(jnp.concatenate(lax.all_to_all(jnp.stack([features] * lax.axis_si...  18.6 us
    dot_general x1, local copies, waits for them, and re-layouts, shards(): jnp.dot(jnp.concatenate(lax.all_to_all(jnp.stack([features] * lax.axis_si...  15.7 us
  transfers between devices with their start and end apart: 1, of which 1 were waited for; matrix products, arithmetic and copies ran while one was open for 4% of the time, Pallas kernels for 0%

profile of v1, /device:TPU:0, one launch (start us, length us, event | category | flops | bytes accessed | tf_op | source)
XLA Modules:
  0.0 428.2 jit_solution(8310165232132085558)
XLA Ops:
  0.0 0.0 copy-start
  0.0 6.8 %stack.5 = bf16[16,1024,512]{2,1,0:T(8,128)(2,1)} broadcast(bf16[1024,512]{1,0:T(8,128)(2,1)} %param.4), dimensions={1,2} | broadcast | bytes 17825792 | tf_op jit(solution)/shard_map/stack | solution.py:41
  6.8 8.0 %all-to-all-start = ((bf16[16,1024,512]{2,1,0:T(8,128)(2,1)}), bf16[16,1024,512]{2,1,0:T(8,128)(2,1)}, u32[]{:S(2)}, u32[]{:S(2)}) async-start(bf16[16,1024,512]{2,1,0:T(8,128)(2,1)} %stack.5), calls=%async_computation | async-start | bytes 33554432 | tf_op jit(solution)/shard_map/all_to_all | solution.py:41
  14.8 0.0 copy-start.2
  14.8 15.7 %copy.15 = bf16[768,8192]{1,0:T(8,128)(2,1)} copy(bf16[768,8192]{0,1:T(8,128)(2,1)} %bitcast.11) | data formatting | bytes 25165824 | tf_op jit(solution)/shard_map/dot_general | solution.py:39
  30.6 0.0 copy-done.2
  30.6 0.1 fusion.3
  30.7 0.2 select_reduce_fusion
  30.9 0.0 copy-done
  30.9 0.2 fusion.4
  31.1 238.9 %all-to-all-done = bf16[16,1024,512]{2,1,0:T(8,128)(2,1)} async-done(((bf16[16,1024,512]{2,1,0:T(8,128)(2,1)}), bf16[16,1024,512]{2,1,0:T(8,128)(2,1)}, u32[]{:S(2)}, u32[]{:S(2)}) %all-to-all-start) | async-done | bytes 16777248 | tf_op jit(solution)/shard_map/all_to_all | solution.py:41
  269.9 18.5 %copy.11 = bf16[1024,16,512]{2,1,0:T(8,128)(2,1)} copy(bf16[1024,16,512]{2,0,1:T(8,128)(2,1)} %bitcast) | data formatting | bytes 33554432 | tf_op jit(solution)/shard_map/reshape | solution.py:40
  288.4 25.6 %reshape.51 = bf16[1024,8192,1,1]{1,0,2,3:T(8,128)(2,1)} reshape(bf16[1024,16,512]{2,1,0:T(8,128)(2,1)} %copy.11) | data formatting | bytes 33554432 | tf_op jit(solution)/shard_map/reshape | solution.py:40
  314.0 18.6 %fusion = f32[1024,3,2,128]{0,3,2,1:T(8,128)S(1)} fusion(bf16[3,2,128,8192]{3,2,1,0:T(8,128)(2,1)} %bitcast.12, bf16[1024,8192,1,1]{1,0,2,3:T(8,128)(2,1)} %reshape.51), kind=kOutput, calls=%fused_computation.1 | convolution fusion | flops 12884901888 | bytes 32505856 | tf_op jit(solution)/shard_map/dot_general | solution.py:39
  332.6 0.2 multiply_reduce_fusion
  332.7 0.1 slice.14
  332.9 0.2 multiply_convert_fusion
  333.1 0.1 pad_maximum_fusion
  333.2 2.2 copy.13
  335.5 1.2 convert_element_type.14
  336.7 4.5 %convolution_convert_fusion = bf16[32,98304]{1,0:T(8,128)(2,1)} fusion(bf16[8,98304]{1,0:T(8,128)(2,1)S(1)} %convert_element_type.14, s32[8]{0:T(128)S(1)} %multiply_add_fusion), kind=kOutput, calls=%fused_computation | convolution fusion | flops 53477632 | bytes 7864352 | tf_op jit(solution)/shard_map/dot_general | solution.py:53
  341.1 7.3 %all_to_all.12 = bf16[8,512,768]{2,1,0:T(8,128)(2,1)} reshape(bf16[32,98304]{1,0:T(8,128)(2,1)} %convolution_convert_fusion) | data formatting | bytes 12582912 | tf_op jit(solution)/shard_map/all_to_all | solution.py:57
  348.4 77.1 %all_to_all.17 = bf16[8,512,768]{2,1,0:T(8,128)(2,1)S(1)} all-to-all(bf16[8,512,768]{2,1,0:T(8,128)(2,1)} %all_to_all.12), channel_id=1, replica_groups=mesh['blk'=16,'tile'=8] {'tile'}, dimensions={0} | all-to-all | bytes 12582912 | tf_op jit(solution)/shard_map/all_to_all | solution.py:57
  425.5 0.0 copy-start.1
  425.5 2.7 copy.17
  428.2 0.0 copy-done.1
  (4 shorter events, 0.1 us)
Async XLA Ops:
  0.0 30.9 %copy-start = (f32[6,128]{1,0:T(8,128)S(1)}, f32[6,128]{1,0:T(8,128)}, u32[]{:S(2)}) copy-start(f32[6,128]{1,0:T(8,128)} %param.6) | copy-start | bytes 9220
  6.8 263.1 %all-to-all-start = ((bf16[16,1024,512]{2,1,0:T(8,128)(2,1)}), bf16[16,1024,512]{2,1,0:T(8,128)(2,1)}, u32[]{:S(2)}, u32[]{:S(2)}) async-start(bf16[16,1024,512]{2,1,0:T(8,128)(2,1)} %stack.5), calls=%async_computation | async-start | bytes 33554432 | tf_op jit(solution)/shard_map/all_to_all | solution.py:41
  14.8 15.7 %copy-start.2 = (s32[8]{0:T(128)S(1)}, s32[8]{0:T(128)}, u32[]{:S(2)}) copy-start(s32[8]{0:T(128)} %param.7) | copy-start | bytes 100
  425.5 2.7 copy-start.1
